TPU v7x, 32 devices: a whole 2x2x4 slice. The times are simulated.
32 devices in a mesh: grp: 2 (over y), band: 8 (over z, x), filt: 2 (over core).
Axes of the slice: x: 2, y: 2, z: 4, core: 2. Of those that a mesh axis runs over, the one named last changes fastest.
Arguments:
- coeff_maps: bfloat16 [128, 64, 512], P(('grp', 'filt'), 'band'), parts along dimension 0, may hold values from -0.75 to 0.75
- image: bfloat16 [6, 64, 512], P('grp', 'band'), parts along dimension 0, may hold values from -24 to 24
- target: bfloat16 [1024, 2, 3, 64, 64], P(('grp', 'band'), None, None, 'filt'), parts along dimension 0, may hold values from -1.5 to 1.5
- dual_rim: float32 [128, 768], P(('grp', 'filt')), parts along dimension 0, may hold values from -18 to 18, as said below
Outputs:
- dict_spectra: bfloat16 [1024, 2, 3, 64, 64], P(('grp', 'band'), None, None, 'filt'), parts along dimension 0
- dictionary: float32 [128, 768], P(('grp', 'filt')), parts along dimension 0
There are 2 independent parts, one for each index of `grp`. A program takes and returns all parts, laid end to end along the dimension named above; each array names one. Nothing has to cross between parts.
Inputs may be any that keep to these rules, and one draw needn't show every extreme that they name: `dual_rim`: a scaled dual variable on the filters' support.
All inputs are finite; a program needn't handle non-finite values.
Results may differ from a plain program's by a relative error of at most 0.0059.
Values may be sent and summed in bfloat16 or wider, within the bound.
No kernel may reach another device: no remote copies, remote signals or barrier semaphores. Data moves between devices by JAX's collectives and lax.ppermute only.
A program may use at most 128 MiB of HBM per device.

v0:
```python
import math
import jax
import jax.numpy as jnp
from jax import lax
from jax.sharding import PartitionSpec as P

K = 16
penalty = 1.0


def forward_columns(length):
    ramp = jnp.arange(length, dtype=jnp.int32)
    phases = ramp[:, None] * ramp[None, :] % length
    angles = phases.astype(jnp.float32) * (2.0 * math.pi / length)
    factor = 1.0 / math.sqrt(length)
    lookup = jnp.stack([jnp.cos(angles) * factor, -jnp.sin(angles) * factor], axis=2)
    return lookup.reshape(length, 2 * length).astype(jnp.bfloat16)


def forward_rows(length):
    ramp = jnp.arange(length, dtype=jnp.int32)
    phases = ramp[:, None] * ramp[None, :] % length
    angles = phases.astype(jnp.float32) * (2.0 * math.pi / length)
    factor = 1.0 / math.sqrt(length)
    return jnp.stack([jnp.cos(angles) * factor, jnp.sin(angles) * factor], axis=0).astype(
        jnp.bfloat16
    )


def inverse_rows(length, width):
    ramp = jnp.arange(length, dtype=jnp.int32)
    reach = jnp.arange(width, dtype=jnp.int32)
    phases = ramp[:, None] * reach[None, :] % length
    angles = phases.astype(jnp.float32) * (2.0 * math.pi / length)
    factor = 1.0 / math.sqrt(length)
    return jnp.stack([jnp.cos(angles) * factor, jnp.sin(angles) * factor], axis=1)


def inverse_columns(length, total_cols, width):
    freqs = jnp.arange(length, dtype=jnp.int32)
    reach = jnp.arange(width, dtype=jnp.int32)
    phases = freqs[:, None] * reach[None, :] % total_cols
    angles = phases.astype(jnp.float32) * (2.0 * math.pi / total_cols)
    factor = 1.0 / math.sqrt(total_cols)
    return jnp.stack([jnp.cos(angles) * factor, jnp.sin(angles) * factor], axis=1)


def spectra(slab_rows, lookup, freqs, members):
    height = slab_rows.shape[0]
    products = jnp.einsum("hk,tgh->ktg", slab_rows, lookup, preferred_element_type=jnp.float32)
    products = products.reshape(freqs, 2, members, 2, height)
    real_part = products[:, 0, :, 0] + products[:, 1, :, 1]
    imag_part = products[:, 1, :, 0] - products[:, 0, :, 1]
    return (real_part, imag_part)


def body(coeff_maps, image, target, dual_rim):
    filters, band_rows, width_cols = coeff_maps.shape
    channels = image.shape[0]
    band_count = lax.axis_size("band")
    height = band_rows * band_count
    per_band = width_cols // band_count
    col_lookup = forward_columns(width_cols)
    row_lookup = forward_rows(height)
    col_maps = jnp.einsum("mrn,nk->rkm", coeff_maps, col_lookup, preferred_element_type=jnp.float32)
    col_maps = col_maps.astype(jnp.bfloat16).reshape(band_rows, 2 * width_cols * filters)
    col_image = jnp.einsum("crn,nk->rkc", image, col_lookup, preferred_element_type=jnp.float32)
    col_image = col_image.astype(jnp.bfloat16).reshape(band_rows, 2 * width_cols * channels)
    got_maps, got_image = (
        lax.all_to_all(col_maps, "band", split_axis=1, concat_axis=0, tiled=True),
        lax.all_to_all(col_image, "band", split_axis=1, concat_axis=0, tiled=True),
    )
    x_re, x_im = spectra(got_maps, row_lookup, per_band, filters)
    s_re, s_im = spectra(got_image, row_lookup, per_band, channels)
    v_full = target.astype(jnp.float32)
    v_re = v_full[:, 0]
    v_im = v_full[:, 1]
    energy = jnp.sum(x_re * x_re + x_im * x_im, axis=1)
    cross_re = jnp.sum(x_re[:, None] * v_re - x_im[:, None] * v_im, axis=2)
    cross_im = jnp.sum(x_re[:, None] * v_im + x_im[:, None] * v_re, axis=2)
    energy, cross_re, cross_im = (
        lax.psum(energy.astype(jnp.bfloat16), "filt").astype(jnp.float32),
        lax.psum(cross_re.astype(jnp.bfloat16), "filt").astype(jnp.float32),
        lax.psum(cross_im.astype(jnp.bfloat16), "filt").astype(jnp.float32),
    )
    denom = penalty + energy[:, None, :]
    coef_re = (s_re - cross_re) / denom
    coef_im = (s_im - cross_im) / denom
    dict_real = v_re + x_re[:, None] * coef_re[:, :, None] + x_im[:, None] * coef_im[:, :, None]
    dict_imag = v_im + x_re[:, None] * coef_im[:, :, None] - x_im[:, None] * coef_re[:, :, None]
    dict_full = jnp.stack([dict_real, dict_imag], axis=1)
    dict_spectra = dict_full.astype(jnp.bfloat16)
    rim_lookup = inverse_rows(height, K)
    folded = jnp.einsum("qpcmg,gty->qpcmty", dict_full, rim_lookup, precision=lax.Precision.HIGHEST)
    rim_real = folded[:, 0, :, :, 0] - folded[:, 1, :, :, 1]
    rim_imag = folded[:, 0, :, :, 1] + folded[:, 1, :, :, 0]
    start_sum = jnp.zeros((filters, channels, K, K), jnp.float32)
    running = start_sum
    pieces = (
        lax.all_gather(rim_real.astype(jnp.bfloat16), "band", axis=0, tiled=True).astype(
            jnp.float32
        ),
        lax.all_gather(rim_imag.astype(jnp.bfloat16), "band", axis=0, tiled=True).astype(
            jnp.float32
        ),
    )
    length = pieces[0].shape[0]
    lookup = inverse_columns(length, width_cols, K)
    running = running + jnp.einsum(
        "qcmy,qx->mcyx", pieces[0], lookup[:, 0], precision=lax.Precision.HIGHEST
    )
    spatial = running - jnp.einsum(
        "qcmy,qx->mcyx", pieces[1], lookup[:, 1], precision=lax.Precision.HIGHEST
    )
    joined = spatial.reshape(filters, channels * K * K) + dual_rim
    spread = jnp.sqrt(jnp.mean(joined * joined, axis=1, keepdims=True))
    dictionary = joined / jnp.maximum(spread, 1.0)
    return (dict_spectra, dictionary)


def solution(mesh):
    placed = (
        P(("grp", "filt"), "band", None),
        P("grp", "band", None),
        P(("grp", "band"), None, None, "filt", None),
        P(("grp", "filt"), None),
    )
    return jax.shard_map(
        body,
        mesh=mesh,
        in_specs=placed,
        out_specs=(P(("grp", "band"), None, None, "filt", None), P(("grp", "filt"), None)),
        check_vma=False,
    )
```

profile of v0, /device:TPU:0, one launch (start us, length us, event | category | flops | bytes accessed | tf_op | source)
XLA Modules:
  0.0 297.8 jit_solution(11534772521772797656)
XLA Ops:
  7.2 0.0 copy-start
  7.2 4.4 %multiply_convert_fusion = (bf16[512,512,1]{1,0,2:T(8,128)(2,1)S(1)}, bf16[512,512,1]{1,0,2:T(8,128)(2,1)S(1)}) fusion(), kind=kLoop, calls=%fused_computation.42 | loop fusion | flops 4980736 | bytes 1048576 | tf_op jit(solution)/shard_map/convert.3
  11.6 0.0 copy-start.5
  11.6 0.1 pad_maximum_fusion.2
  11.7 1.0 copy.59
  12.7 0.4 convert_element_type.110
  13.1 0.0 copy-done.5
  13.1 0.4 fusion.15
  13.5 0.7 copy.69
  14.2 0.6 all_to_all.32
  14.9 0.9 copy.70
  15.7 7.3 %all-to-all-start.1 = ((bf16[8,8,384]{2,0,1:T(8,128)(2,1)}), bf16[8,8,384]{2,0,1:T(8,128)(2,1)S(1)}, u32[]{:S(2)}, u32[]{:S(2)}) async-start(bf16[8,8,384]{2,0,1:T(8,128)(2,1)} %copy.70), calls=%async_computation.1 | async-start | bytes 98304 | tf_op jit(solution)/shard_map/all_to_all | solution.py:71
  23.0 0.0 copy-done
  23.0 0.5 fusion.11
  23.5 1.0 copy.62
  24.5 2.3 all_to_all.28
  26.8 1.1 copy.63
  27.9 1.9 all-to-all-done.1
  29.8 4.1 %all-to-all-start = ((bf16[8,8,4096]{2,0,1:T(8,128)(2,1)}), bf16[8,8,4096]{2,0,1:T(8,128)(2,1)S(1)}, u32[]{:S(2)}, u32[]{:S(2)}) async-start(bf16[8,8,4096]{2,0,1:T(8,128)(2,1)} %copy.63), calls=%async_computation | async-start | bytes 1048576 | tf_op jit(solution)/shard_map/all_to_all | solution.py:70
  33.9 0.0 all-gather.7.cloned.1.call-start
  33.9 0.1 sine_multiply_fusion
  34.0 0.2 multiply_convert_fusion.2
  34.1 6.4 %copy_convert_fusion = f32[64,2,3,32,64]{4,0,3,2,1:T(8,128)} fusion(bf16[64,2,3,32,64]{4,3,2,1,0:T(8,128)(2,1)} %param.6), kind=kLoop, calls=%fused_computation.12 | loop fusion | flops 786432 | bytes 4718592 | tf_op jit(solution)/shard_map/convert_element_type | solution.py:75
  40.5 0.1 copy.71
  40.6 0.1 dot_general.35
  40.7 0.2 fusion.39
  40.9 6.9 %all-to-all-done = bf16[8,8,4096]{2,0,1:T(8,128)(2,1)S(1)} async-done(((bf16[8,8,4096]{2,0,1:T(8,128)(2,1)}), bf16[8,8,4096]{2,0,1:T(8,128)(2,1)S(1)}, u32[]{:S(2)}, u32[]{:S(2)}) %all-to-all-start) | async-done | bytes 524320 | tf_op jit(solution)/shard_map/all_to_all | solution.py:70
  47.9 0.5 copy.64
  48.3 0.0 slice-start
  48.3 0.0 slice-start.1
  48.4 0.9 fusion.22
  49.2 0.7 add_reduce_fusion
  49.9 0.0 copy-start.2
  49.9 0.0 copy-start.3
  49.9 0.6 slice-done
  50.5 1.4 slice-done.1
  51.9 1.1 fusion.4
  53.0 0.0 copy-done.2
  53.0 0.0 copy-done.3
  53.0 3.9 %all-reduce = (bf16[64,3,64]{2,0,1:T(8,128)(2,1)S(1)}, bf16[64,64]{1,0:T(8,128)(2,1)S(1)}, bf16[64,3,64]{2,0,1:T(8,128)(2,1)S(1)}) all-reduce(bf16[64,3,64]{2,0,1:T(8,128)(2,1)S(1)} %get-tuple-element.11, bf16[64,64]{1,0:T(8,128)(2,1)S(1)} %get-tuple-element.17, ...), channel_id=1, replica_groups=mesh['grp'=2,'band'=8,'filt'=2] {'filt'}, use_global_device_ids=true, to_apply=%region_5.6 | all-reduce | flops 28672 | bytes 114688 | tf_op jit(solution)/shard_map/psum | solution.py:84
  57.0 4.5 %multiply_add_fusion = (f32[64,1,3,32,64]{4,0,3,2,1:T(8,128)S(1)}, f32[64,1,3,32,64]{4,0,3,2,1:T(8,128)S(1)}) fusion(f32[64,2,3,32,64]{4,0,3,2,1:T(8,128)} %copy_convert_fusion, f32[64,3,64]{2,0,1:T(8,128)S(1)} %get-tuple-element.25, f32[64,32,64]{2,0,1:T(8,128)} %copy-done.3, f32[64,3,64]{2,0,1:T(8,128)S(1)} %get-tuple-element.24, f32[64,32,64]{2,0,1:T(8,128)} %copy-done.2), kind=kLoop, calls=%fused_computation.14 | loop fusion | flops 3145728 | bytes 7438336 | tf_op jit(solution)/shard_map/add | solution.py:89
  61.5 0.0 copy-start.1
  61.5 17.3 %fusion = f32[64,2,3,32,2,16]{0,5,4,3,2,1:T(8,128)S(1)} fusion(f32[64,1,3,32,64]{4,0,3,2,1:T(8,128)S(1)} %get-tuple-element.21, f32[64,1,3,32,64]{4,0,3,2,1:T(8,128)S(1)} %get-tuple-element.20, f32[64,1,16]{0,2,1:T(8,128)S(1)} %get-tuple-element.30, f32[64,1,16]{0,2,1:T(8,128)S(1)} %get-tuple-element.31), kind=kOutput, calls=%fused_computation.1 | convolution fusion | flops 302778368 | bytes 4726784 | tf_op jit(solution)/shard_map/qpcmg,gty->qpcmty/dot_general | solution.py:94
  78.9 0.0 copy-done.1
  78.9 1.1 fusion.30
  80.0 2.7 copy.77
  82.7 0.0 all-gather.7.cloned.1.call-update
  82.7 0.3 all-gather.5.cloned.1.call-start
  83.0 2.7 copy.75
  85.7 0.0 all-gather.5.cloned.1.call-update
  85.7 2.4 fusion.2
  88.1 3.7 %copy.80 = bf16[64,2,3,32,64]{4,3,2,1,0:T(8,128)(2,1)} copy(bf16[64,2,3,32,64]{4,0,3,2,1:T(8,128)(2,1)S(1)} %fusion.2) | data formatting | bytes 3145728
  91.7 89.3 %all-gather.7.cloned.1.call-done = bf16[512,1,3,32,1,16]{3,5,4,2,1,0:T(8,128)(2,1)} async-done(((bf16[64,1,3,32,1,16]{3,5,4,2,1,0:T(8,128)(2,1)}), bf16[512,1,3,32,1,16]{3,5,4,2,1,0:T(8,128)(2,1)}) %all-gather.7.cloned.1.call-update) | async-done | bytes 1572880 | tf_op jit(solution)/shard_map/all_gather | solution.py:103
  181.0 6.4 %copy.78 = bf16[512,1,3,32,1,16]{0,3,5,2,4,1:T(8,128)(2,1)S(1)} copy(bf16[512,1,3,32,1,16]{3,5,4,2,1,0:T(8,128)(2,1)} %all-gather.7.cloned.1.call-done) | data formatting | bytes 3145728 | tf_op jit(solution)/shard_map/all_gather | solution.py:103
  187.4 3.2 %fusion.7 = f32[16,3,32,16]{2,0,3,1:T(8,128)S(1)} fusion(bf16[512,1,3,32,1,16]{0,3,5,2,4,1:T(8,128)(2,1)S(1)} %copy.78), kind=kOutput, calls=%fused_computation.15 | convolution fusion | flops 151117824 | bytes 1671168 | tf_op jit(solution)/shard_map/qcmy,qx->mcyx/dot_general | solution.py:112
  190.5 0.0 copy-start.4
  190.5 89.9 %all-gather.5.cloned.1.call-done = bf16[512,1,3,32,1,16]{3,5,4,2,1,0:T(8,128)(2,1)} async-done(((bf16[64,1,3,32,1,16]{3,5,4,2,1,0:T(8,128)(2,1)}), bf16[512,1,3,32,1,16]{3,5,4,2,1,0:T(8,128)(2,1)}) %all-gather.5.cloned.1.call-update) | async-done | bytes 1572880 | tf_op jit(solution)/shard_map/all_gather | solution.py:100
  280.4 6.4 %copy.76 = bf16[512,1,3,32,1,16]{0,3,5,2,4,1:T(8,128)(2,1)S(1)} copy(bf16[512,1,3,32,1,16]{3,5,4,2,1,0:T(8,128)(2,1)} %all-gather.5.cloned.1.call-done) | data formatting | bytes 3145728 | tf_op jit(solution)/shard_map/all_gather | solution.py:100
  286.8 3.2 %fusion.12 = f32[16,3,32,16]{2,0,3,1:T(8,128)S(1)} fusion(f32[16,3,32,16]{2,0,3,1:T(8,128)S(1)} %fusion.7, bf16[512,1,3,32,1,16]{0,3,5,2,4,1:T(8,128)(2,1)S(1)} %copy.76), kind=kOutput, calls=%fused_computation.24 | convolution fusion | flops 151142400 | bytes 1769472 | tf_op jit(solution)/shard_map/qcmy,qx->mcyx/dot_general | solution.py:109
  290.0 0.2 copy.79
  290.1 0.0 copy-done.4
  290.1 0.1 multiply_reduce_fusion
  290.3 0.7 broadcast_divide_fusion
  (4 shorter events, 0.1 us)
Async XLA Ops:
  7.2 15.8 %copy-start = (bf16[32,8,512]{2,1,0:T(8,128)(2,1)S(1)}, bf16[32,8,512]{2,1,0:T(8,128)(2,1)}, u32[]{:S(2)}) copy-start(bf16[32,8,512]{2,1,0:T(8,128)(2,1)} %param.4) | copy-start | bytes 786436
  11.6 1.6 copy-start.5
  15.7 14.0 %all-to-all-start.1 = ((bf16[8,8,384]{2,0,1:T(8,128)(2,1)}), bf16[8,8,384]{2,0,1:T(8,128)(2,1)S(1)}, u32[]{:S(2)}, u32[]{:S(2)}) async-start(bf16[8,8,384]{2,0,1:T(8,128)(2,1)} %copy.70), calls=%async_computation.1 | async-start | bytes 98304 | tf_op jit(solution)/shard_map/all_to_all | solution.py:71
  29.8 18.1 %all-to-all-start = ((bf16[8,8,4096]{2,0,1:T(8,128)(2,1)}), bf16[8,8,4096]{2,0,1:T(8,128)(2,1)S(1)}, u32[]{:S(2)}, u32[]{:S(2)}) async-start(bf16[8,8,4096]{2,0,1:T(8,128)(2,1)} %copy.63), calls=%async_computation | async-start | bytes 1048576 | tf_op jit(solution)/shard_map/all_to_all | solution.py:70
  33.9 147.1 %all-gather.7.cloned.1.call-start = ((), (), s32[]{:S(2)}) async-start(), calls=%async_computation.3 | async-start | bytes 7077888 | tf_op jit(solution)/shard_map/all_gather | solution.py:103
  48.3 2.2 slice-start
  48.3 3.6 %slice-start.1 = ((s8[6291456]{0:T(1024)(128)(4,1)}), s8[2097152]{0:T(1024)(128)(4,1)S(1)}, s32[]{:S(2)}) async-start(s8[6291456]{0:T(1024)(128)(4,1)} %bitcast.128), calls=%async_computation.5 | async-start | bytes 4194304
  49.9 3.1 %copy-start.2 = (f32[64,32,64]{2,0,1:T(8,128)}, f32[64,32,64]{2,0,1:T(8,128)S(1)}, u32[]{:S(2)}) copy-start(f32[64,32,64]{2,0,1:T(8,128)S(1)} %get-tuple-element.18) | copy-start | bytes 1572868
  49.9 3.1 %copy-start.3 = (f32[64,32,64]{2,0,1:T(8,128)}, f32[64,32,64]{2,0,1:T(8,128)S(1)}, u32[]{:S(2)}) copy-start(f32[64,32,64]{2,0,1:T(8,128)S(1)} %get-tuple-element.19) | copy-start | bytes 1572868
  61.5 17.4 %copy-start.1 = (f32[64,1,3,32,64]{4,0,3,2,1:T(8,128)}, f32[64,1,3,32,64]{4,0,3,2,1:T(8,128)S(1)}, u32[]{:S(2)}) copy-start(f32[64,1,3,32,64]{4,0,3,2,1:T(8,128)S(1)} %get-tuple-element.21) | copy-start | bytes 4718596
  82.7 197.7 %all-gather.5.cloned.1.call-start = ((), (), s32[]{:S(2)}) async-start(), calls=%async_computation.2 | async-start | bytes 7077888 | tf_op jit(solution)/shard_map/all_gather | solution.py:100
  190.5 99.6 %copy-start.4 = (f32[32,768]{1,0:T(8,128)S(1)}, f32[32,768]{1,0:T(8,128)}, u32[]{:S(2)}) copy-start(f32[32,768]{1,0:T(8,128)} %param.7) | copy-start | bytes 294916
Sparse Core Ops, SparseCore 0:
  82.9 98.1 all-gather.6
  183.2 97.1 all-gather.4
where the time goes:
time: 298 us
  waiting for transfers between devices  188 us (63%)
  local copies, waits for them, and re-layouts  32.7 us (11%)
  matrix products  25.6 us (9%)
  other arithmetic  21.7 us (7%)
  between operations  14.3 us (5%)
  starting transfers between devices  11.6 us (4%)
  blocking collectives  3.9 us (1%)
    all_gather x1, waiting for transfers between devices, body(): lax.all_gather(rim_real.astype(jnp.bfloat16), 'band', axis=0, tiled=True)  89.9 us
    all_gather x1, waiting for transfers between devices, body(): lax.all_gather(rim_imag.astype(jnp.bfloat16), 'band', axis=0, tiled=True)  89.3 us
    dot_general x1, matrix products, body(): jnp.einsum('qpcmg,gty->qpcmty', dict_full, rim_lookup, precision=lax.Prec...  17.3 us
    all_to_all x1, starting transfers between devices, body(): lax.all_to_all(col_image, 'band', split_axis=1, concat_axis=0, tiled=True)  7.25 us
    all_to_all x1, waiting for transfers between devices, body(): lax.all_to_all(col_maps, 'band', split_axis=1, concat_axis=0, tiled=True)  6.91 us
    convert_element_type x1, other arithmetic, body(): v_full = target.astype(jnp.float32)  6.37 us
    all_gather x1, local copies, waits for them, and re-layouts, body(): lax.all_gather(rim_imag.astype(jnp.bfloat16), 'band', axis=0, tiled=True)  6.36 us
    all_gather x1, local copies, waits for them, and re-layouts, body(): lax.all_gather(rim_real.astype(jnp.bfloat16), 'band', axis=0, tiled=True)  6.36 us
  transfers between devices with their start and end apart: 4, of which 4 were waited for; matrix products, arithmetic and copies ran while one was open for 9% of the time, Pallas kernels for 0%

commit v1 on v0

--- a/solution.py
+++ b/solution.py
@@ -6,6 +6,17 @@
 
 K = 16
 penalty = 1.0
+
+
+def do_the_zone(frame, pos_dim, xx):
+    y1, mid_arr = (frame.shape[:pos_dim], frame.shape[pos_dim + 1 :])
+    return jnp.moveaxis(frame.reshape(*y1, xx, -1, *mid_arr), pos_dim, 0)
+
+
+def keep_up_outputs(a0, where_dim):
+    a0 = jnp.moveaxis(a0, 0, where_dim)
+    y2 = a0.shape
+    return a0.reshape(*y2[:where_dim], y2[where_dim] * y2[where_dim + 1], *y2[where_dim + 2 :])
 
 
 def forward_columns(length):
@@ -66,8 +77,24 @@
     col_maps = col_maps.astype(jnp.bfloat16).reshape(band_rows, 2 * width_cols * filters)
     col_image = jnp.einsum("crn,nk->rkc", image, col_lookup, preferred_element_type=jnp.float32)
     col_image = col_image.astype(jnp.bfloat16).reshape(band_rows, 2 * width_cols * channels)
+
+    def launch_the_spots(patch, axis_tag, w_in, local_x):
+        then = lax.axis_index(axis_tag)
+        item_now = lax.axis_size(axis_tag)
+        g_now, x_next = (item_now, then)
+        high = do_the_zone(patch, w_in, g_now)
+        odd = high
+        for i in range(1, g_now):
+            passed, b_now = ((x_next + i) % g_now, (x_next - i) % g_now)
+            front = lax.dynamic_index_in_dim(high, passed, 0)
+            z = map(lambda dd: (dd, (dd + i) % g_now), range(g_now))
+            now = list(z)
+            v1 = lax.ppermute(front, axis_name=axis_tag, perm=now)
+            odd = lax.dynamic_update_slice_in_dim(odd, v1, b_now, axis=0)
+        return keep_up_outputs(odd, local_x)
+
     got_maps, got_image = (
-        lax.all_to_all(col_maps, "band", split_axis=1, concat_axis=0, tiled=True),
+        launch_the_spots(col_maps, "band", 1, local_x=0),
         lax.all_to_all(col_image, "band", split_axis=1, concat_axis=0, tiled=True),
     )
     x_re, x_im = spectra(got_maps, row_lookup, per_band, filters)

time: 298 us -> 315 us (1.057)
  local copies, waits for them, and re-layouts: 32.7 us -> 49 us
  waiting for transfers between devices: 188 us -> 178 us
  starting transfers between devices: 11.6 us -> 19.7 us
    ppermute x0 -> x7, starting transfers between devices: none -> 16.1 us  [launch_the_spots(): v1 = lax.ppermute(front, axis_name=axis_tag, perm=now)]
    dynamic_update_slice x0 -> x8, local copies, waits for them, and re-layouts: none -> 15.2 us  [launch_the_spots(): odd = lax.dynamic_update_slice_in_dim(odd, v1, b_now, axis=0)]
    all_to_all x1 -> x0, waiting for transfers between devices: 6.91 us -> none  [body(): lax.all_to_all(col_maps, 'band', split_axis=1, concat_axis=0, tiled=True)]
    all_to_all x1 -> x0, starting transfers between devices: 4.1 us -> none  [body(): lax.all_to_all(col_maps, 'band', split_axis=1, concat_axis=0, tiled=True)]
    all_to_all x1, starting transfers between devices: 7.25 us -> 3.35 us  [body(): lax.all_to_all(col_image, 'band', split_axis=1, concat_axis=0, tiled=True)]
    all_to_all x2 -> x0, local copies, waits for them, and re-layouts: 3.35 us -> none  [body(): lax.all_to_all(col_maps, 'band', split_axis=1, concat_axis=0, tiled=True)]
  transfers between devices with their start and end apart: 4 -> 10, of which waited for: 4 -> 2; matrix products, arithmetic and copies ran while one was open for 9% -> 15% of each run, Pallas kernels for 0% -> 0%
where the time goes in v1:
time: 315 us; the launch traced here: 314 us
  waiting for transfers between devices  178 us (57%)
  local copies, waits for them, and re-layouts  49 us (16%)
  matrix products  26.9 us (9%)
  other arithmetic  21.7 us (7%)
  starting transfers between devices  19.7 us (6%)
  between operations  14.7 us (5%)
  blocking collectives  3.72 us (1%)
    all_gather x1, waiting for transfers between devices, body(): lax.all_gather(rim_real.astype(jnp.bfloat16), 'band', axis=0, tiled=True)  89.9 us
    all_gather x1, waiting for transfers between devices, body(): lax.all_gather(rim_imag.astype(jnp.bfloat16), 'band', axis=0, tiled=True)  88.4 us
    dot_general x1, matrix products, body(): jnp.einsum('qpcmg,gty->qpcmty', dict_full, rim_lookup, precision=lax.Prec...  17.3 us
    ppermute x7, starting transfers between devices, launch_the_spots(): v1 = lax.ppermute(front, axis_name=axis_tag, perm=now)  16.1 us
    dynamic_update_slice x8, local copies, waits for them, and re-layouts, launch_the_spots(): odd = lax.dynamic_update_slice_in_dim(odd, v1, b_now, axis=0)  15.2 us
    unnamed x17, local copies, waits for them, and re-layouts  6.73 us
    convert_element_type x1, other arithmetic, body(): v_full = target.astype(jnp.float32)  6.38 us
    all_gather x1, local copies, waits for them, and re-layouts, body(): lax.all_gather(rim_imag.astype(jnp.bfloat16), 'band', axis=0, tiled=True)  6.36 us
  transfers between devices with their start and end apart: 10, of which 2 were waited for; matrix products, arithmetic and copies ran while one was open for 15% of the time, Pallas kernels for 0%

profile of v1, /device:TPU:0, one launch (start us, length us, event | category | flops | bytes accessed | tf_op | source)
XLA Modules:
  0.0 313.9 jit_solution(11351707331705280978)
XLA Ops:
  7.2 0.0 copy-start
  7.3 4.4 %multiply_convert_fusion = (bf16[512,512,1]{1,0,2:T(8,128)(2,1)S(1)}, bf16[512,512,1]{1,0,2:T(8,128)(2,1)S(1)}) fusion(), kind=kLoop, calls=%fused_computation.42 | loop fusion | flops 4980736 | bytes 1048576 | tf_op jit(solution)/shard_map/convert.3
  11.7 0.1 pad_maximum_fusion.2
  11.8 1.0 copy.59
  12.8 0.4 convert_element_type.110
  13.2 1.0 copy-done.4
  14.2 0.5 fusion.11
  14.7 1.0 copy.62
  15.7 2.3 reshape_reshape.3
  18.0 1.2 dynamic-slice_bitcast_fusion
  19.2 3.0 collective-permute-start
  22.2 1.6 collective-permute-start.1
  23.8 2.6 collective-permute-start.2
  26.3 1.2 collective-permute-start.3
  27.6 2.6 collective-permute-start.4
  30.2 1.6 fusion.15
  31.8 0.7 copy.69
  32.5 0.6 all_to_all.14
  33.1 0.9 copy.70
  34.0 3.3 %all-to-all-start = ((bf16[8,8,384]{2,0,1:T(8,128)(2,1)}), bf16[8,8,384]{2,0,1:T(8,128)(2,1)S(1)}, u32[]{:S(2)}, u32[]{:S(2)}) async-start(bf16[8,8,384]{2,0,1:T(8,128)(2,1)} %copy.70), calls=%async_computation | async-start | bytes 98304 | tf_op jit(solution)/shard_map/all_to_all | solution.py:98
  37.4 0.0 all-gather.7.cloned.1.call-start
  37.5 6.4 %copy_convert_fusion = f32[64,2,3,32,64]{4,0,3,2,1:T(8,128)} fusion(bf16[64,2,3,32,64]{4,3,2,1,0:T(8,128)(2,1)} %param.6), kind=kLoop, calls=%fused_computation.12 | loop fusion | flops 786432 | bytes 4718592 | tf_op jit(solution)/shard_map/convert_element_type | solution.py:102
  43.9 0.2 multiply_convert_fusion.2
  44.1 3.6 %collective-permute-start.5 = (bf16[1,8,4096]{2,0,1:T(2,128)(2,1)S(1)}, bf16[1,8,4096]{2,0,1:T(2,128)(2,1)S(1)}, u32[]{:S(2)}, u32[]{:S(2)}) collective-permute-start(bf16[1,8,4096]{2,0,1:T(2,128)(2,1)S(1)} %get-tuple-element.25), channel_id=1, source_target_pairs={{0,12},{2,14},{4,0},{6,2},{8,4},{10,6},{12,8},{14,10},{1,13},{3,15... | collective-permute-start | bytes 196616 | tf_op jit(solution)/shard_map/ppermute | solution.py:92
  47.7 1.5 collective-permute-start.6
  49.2 0.1 sine_multiply_fusion
  49.2 2.5 dynamic_update_slice.21
  51.7 2.5 dynamic_update_slice.22
  54.2 2.5 dynamic_update_slice.23
  56.7 2.5 dynamic_update_slice.24
  59.2 2.5 dynamic_update_slice.25
  61.7 1.3 dynamic_update_slice.26
  63.0 1.3 dynamic_update_slice.27
  64.3 0.3 copy.108
  64.6 0.5 copy.64
  65.1 0.9 fusion.22
  66.0 0.7 add_reduce_fusion
  66.6 0.6 slice-done
  67.3 1.4 slice-done.1
  68.7 1.1 fusion.4
  69.8 3.7 %all-reduce = (bf16[64,3,64]{2,0,1:T(8,128)(2,1)S(1)}, bf16[64,64]{1,0:T(8,128)(2,1)S(1)}, bf16[64,3,64]{2,0,1:T(8,128)(2,1)S(1)}) all-reduce(bf16[64,3,64]{2,0,1:T(8,128)(2,1)S(1)} %get-tuple-element.11, bf16[64,64]{1,0:T(8,128)(2,1)S(1)} %get-tuple-element.17, ...), channel_id=1, replica_groups=mesh['grp'=2,'band'=8,'filt'=2] {'filt'}, use_global_device_ids=true, to_apply=%region_5.6 | all-reduce | flops 28672 | bytes 114688 | tf_op jit(solution)/shard_map/psum | solution.py:111
  73.5 0.1 copy.71
  73.6 0.1 dot_general.35
  73.7 0.2 fusion.39
  74.0 4.5 %multiply_add_fusion = (f32[64,1,3,32,64]{4,0,3,2,1:T(8,128)S(1)}, f32[64,1,3,32,64]{4,0,3,2,1:T(8,128)S(1)}) fusion(f32[64,2,3,32,64]{4,0,3,2,1:T(8,128)} %copy_convert_fusion, f32[64,3,64]{2,0,1:T(8,128)S(1)} %get-tuple-element.32, f32[64,32,64]{2,0,1:T(8,128)} %copy-done.3, f32[64,3,64]{2,0,1:T(8,128)S(1)} %get-tuple-element.31, f32[64,32,64]{2,0,1:T(8,128)} %copy-done.2), kind=kLoop, calls=%fused_computation.14 | loop fusion | flops 3145728 | bytes 7438336 | tf_op jit(solution)/shard_map/add | solution.py:116
  78.5 17.3 %fusion = f32[64,2,3,32,2,16]{0,5,4,3,2,1:T(8,128)S(1)} fusion(f32[64,1,3,32,64]{4,0,3,2,1:T(8,128)S(1)} %get-tuple-element.21, f32[64,1,3,32,64]{4,0,3,2,1:T(8,128)S(1)} %get-tuple-element.20, f32[64,1,16]{0,2,1:T(8,128)S(1)} %get-tuple-element.37, f32[64,1,16]{0,2,1:T(8,128)S(1)} %get-tuple-element.38), kind=kOutput, calls=%fused_computation.1 | convolution fusion | flops 302778368 | bytes 4726784 | tf_op jit(solution)/shard_map/qpcmg,gty->qpcmty/dot_general | solution.py:121
  95.8 0.0 copy-done.1
  95.9 1.1 fusion.30
  97.0 2.7 copy.77
  99.7 0.0 all-gather.7.cloned.1.call-update
  99.7 0.3 all-gather.5.cloned.1.call-start
  100.0 2.7 copy.75
  102.6 0.0 all-gather.5.cloned.1.call-update
  102.7 2.4 fusion.2
  105.0 3.7 %copy.80 = bf16[64,2,3,32,64]{4,3,2,1,0:T(8,128)(2,1)} copy(bf16[64,2,3,32,64]{4,0,3,2,1:T(8,128)(2,1)S(1)} %fusion.2) | data formatting | bytes 3145728
  108.7 88.4 %all-gather.7.cloned.1.call-done = bf16[512,1,3,32,1,16]{3,5,4,2,1,0:T(8,128)(2,1)} async-done(((bf16[64,1,3,32,1,16]{3,5,4,2,1,0:T(8,128)(2,1)}), bf16[512,1,3,32,1,16]{3,5,4,2,1,0:T(8,128)(2,1)}) %all-gather.7.cloned.1.call-update) | async-done | bytes 1572880 | tf_op jit(solution)/shard_map/all_gather | solution.py:130
  197.1 6.4 %copy.78 = bf16[512,1,3,32,1,16]{0,3,5,2,4,1:T(8,128)(2,1)S(1)} copy(bf16[512,1,3,32,1,16]{3,5,4,2,1,0:T(8,128)(2,1)} %all-gather.7.cloned.1.call-done) | data formatting | bytes 3145728 | tf_op jit(solution)/shard_map/all_gather | solution.py:130
  203.5 3.2 %fusion.7 = f32[16,3,32,16]{2,0,3,1:T(8,128)S(1)} fusion(bf16[512,1,3,32,1,16]{0,3,5,2,4,1:T(8,128)(2,1)S(1)} %copy.78), kind=kOutput, calls=%fused_computation.15 | convolution fusion | flops 151117824 | bytes 1671168 | tf_op jit(solution)/shard_map/qcmy,qx->mcyx/dot_general | solution.py:139
  206.6 89.9 %all-gather.5.cloned.1.call-done = bf16[512,1,3,32,1,16]{3,5,4,2,1,0:T(8,128)(2,1)} async-done(((bf16[64,1,3,32,1,16]{3,5,4,2,1,0:T(8,128)(2,1)}), bf16[512,1,3,32,1,16]{3,5,4,2,1,0:T(8,128)(2,1)}) %all-gather.5.cloned.1.call-update) | async-done | bytes 1572880 | tf_op jit(solution)/shard_map/all_gather | solution.py:127
  296.5 6.4 %copy.76 = bf16[512,1,3,32,1,16]{0,3,5,2,4,1:T(8,128)(2,1)S(1)} copy(bf16[512,1,3,32,1,16]{3,5,4,2,1,0:T(8,128)(2,1)} %all-gather.5.cloned.1.call-done) | data formatting | bytes 3145728 | tf_op jit(solution)/shard_map/all_gather | solution.py:127
  302.9 3.2 %fusion.12 = f32[16,3,32,16]{2,0,3,1:T(8,128)S(1)} fusion(f32[16,3,32,16]{2,0,3,1:T(8,128)S(1)} %fusion.7, bf16[512,1,3,32,1,16]{0,3,5,2,4,1:T(8,128)(2,1)S(1)} %copy.76), kind=kOutput, calls=%fused_computation.24 | convolution fusion | flops 151142400 | bytes 1769472 | tf_op jit(solution)/shard_map/qcmy,qx->mcyx/dot_general | solution.py:136
  306.1 0.2 copy.79
  306.2 0.1 multiply_reduce_fusion
  306.4 0.7 broadcast_divide_fusion
  (23 shorter events, 0.1 us)
Async XLA Ops:
  7.2 7.0 %copy-start = (bf16[32,8,512]{2,1,0:T(8,128)(2,1)S(1)}, bf16[32,8,512]{2,1,0:T(8,128)(2,1)}, u32[]{:S(2)}) copy-start(bf16[32,8,512]{2,1,0:T(8,128)(2,1)} %param.4) | copy-start | bytes 786436
  13.2 1.0 copy-start.4
  19.2 24.9 %collective-permute-start = (bf16[1,8,4096]{2,0,1:T(2,128)(2,1)S(1)}, bf16[1,8,4096]{2,0,1:T(2,128)(2,1)}, u32[]{:S(2)}, u32[]{:S(2)}) collective-permute-start(bf16[1,8,4096]{2,0,1:T(2,128)(2,1)S(1)} %get-tuple-element.30), channel_id=1, source_target_pairs={{0,2},{2,4},{4,6},{6,8},{8,10},{10,12},{12,14},{14,0},{1,3},{3,5},... | collective-permute-start | bytes 196616 | tf_op jit(solution)/shard_map/ppermute | solution.py:92
  22.2 25.5 %collective-permute-start.1 = (bf16[1,8,4096]{2,0,1:T(2,128)(2,1)S(1)}, bf16[1,8,4096]{2,0,1:T(2,128)(2,1)}, u32[]{:S(2)}, u32[]{:S(2)}) collective-permute-start(bf16[1,8,4096]{2,0,1:T(2,128)(2,1)S(1)} %get-tuple-element.29), channel_id=1, source_target_pairs={{0,4},{2,6},{4,8},{6,10},{8,12},{10,14},{12,0},{14,2},{1,5},{3,7},... | collective-permute-start | bytes 196616 | tf_op jit(solution)/shard_map/ppermute | solution.py:92
  23.8 30.4 %collective-permute-start.2 = (bf16[1,8,4096]{2,0,1:T(2,128)(2,1)S(1)}, bf16[1,8,4096]{2,0,1:T(2,128)(2,1)}, u32[]{:S(2)}, u32[]{:S(2)}) collective-permute-start(bf16[1,8,4096]{2,0,1:T(2,128)(2,1)S(1)} %get-tuple-element.28), channel_id=1, source_target_pairs={{0,6},{2,8},{4,10},{6,12},{8,14},{10,0},{12,2},{14,4},{1,7},{3,9},... | collective-permute-start | bytes 196616 | tf_op jit(solution)/shard_map/ppermute | solution.py:92
  26.3 30.3 %collective-permute-start.3 = (bf16[1,8,4096]{2,0,1:T(2,128)(2,1)S(1)}, bf16[1,8,4096]{2,0,1:T(2,128)(2,1)}, u32[]{:S(2)}, u32[]{:S(2)}) collective-permute-start(bf16[1,8,4096]{2,0,1:T(2,128)(2,1)S(1)} %get-tuple-element.27), channel_id=1, source_target_pairs={{0,8},{2,10},{4,12},{6,14},{8,0},{10,2},{12,4},{14,6},{1,9},{3,11}... | collective-permute-start | bytes 196616 | tf_op jit(solution)/shard_map/ppermute | solution.py:92
  27.6 31.6 %collective-permute-start.4 = (bf16[1,8,4096]{2,0,1:T(2,128)(2,1)S(1)}, bf16[1,8,4096]{2,0,1:T(2,128)(2,1)}, u32[]{:S(2)}, u32[]{:S(2)}) collective-permute-start(bf16[1,8,4096]{2,0,1:T(2,128)(2,1)S(1)} %get-tuple-element.26), channel_id=1, source_target_pairs={{0,10},{2,12},{4,14},{6,0},{8,2},{10,4},{12,6},{14,8},{1,11},{3,13... | collective-permute-start | bytes 196616 | tf_op jit(solution)/shard_map/ppermute | solution.py:92
  34.0 39.5 %all-to-all-start = ((bf16[8,8,384]{2,0,1:T(8,128)(2,1)}), bf16[8,8,384]{2,0,1:T(8,128)(2,1)S(1)}, u32[]{:S(2)}, u32[]{:S(2)}) async-start(bf16[8,8,384]{2,0,1:T(8,128)(2,1)} %copy.70), calls=%async_computation | async-start | bytes 98304 | tf_op jit(solution)/shard_map/all_to_all | solution.py:98
  37.4 159.7 %all-gather.7.cloned.1.call-start = ((), (), s32[]{:S(2)}) async-start(), calls=%async_computation.2 | async-start | bytes 7077888 | tf_op jit(solution)/shard_map/all_gather | solution.py:130
  44.1 17.6 %collective-permute-start.5 = (bf16[1,8,4096]{2,0,1:T(2,128)(2,1)S(1)}, bf16[1,8,4096]{2,0,1:T(2,128)(2,1)S(1)}, u32[]{:S(2)}, u32[]{:S(2)}) collective-permute-start(bf16[1,8,4096]{2,0,1:T(2,128)(2,1)S(1)} %get-tuple-element.25), channel_id=1, source_target_pairs={{0,12},{2,14},{4,0},{6,2},{8,4},{10,6},{12,8},{14,10},{1,13},{3,15... | collective-permute-start | bytes 196616 | tf_op jit(solution)/shard_map/ppermute | solution.py:92
  47.7 15.3 %collective-permute-start.6 = (bf16[1,8,4096]{2,0,1:T(2,128)(2,1)S(1)}, bf16[1,8,4096]{2,0,1:T(2,128)(2,1)S(1)}, u32[]{:S(2)}, u32[]{:S(2)}) collective-permute-start(bf16[1,8,4096]{2,0,1:T(2,128)(2,1)S(1)} %get-tuple-element.24), channel_id=1, source_target_pairs={{0,14},{2,0},{4,2},{6,4},{8,6},{10,8},{12,10},{14,12},{1,15},{3,1}... | collective-permute-start | bytes 196616 | tf_op jit(solution)/shard_map/ppermute | solution.py:92
  65.1 2.2 slice-start
  65.1 3.6 %slice-start.1 = ((s8[6291456]{0:T(1024)(128)(4,1)}), s8[2097152]{0:T(1024)(128)(4,1)S(1)}, s32[]{:S(2)}) async-start(s8[6291456]{0:T(1024)(128)(4,1)} %bitcast.143), calls=%async_computation.4 | async-start | bytes 4194304
  66.6 3.1 copy-start.2
  66.6 3.1 copy-start.3
  78.5 17.4 %copy-start.1 = (f32[64,1,3,32,64]{4,0,3,2,1:T(8,128)}, f32[64,1,3,32,64]{4,0,3,2,1:T(8,128)S(1)}, u32[]{:S(2)}) copy-start(f32[64,1,3,32,64]{4,0,3,2,1:T(8,128)S(1)} %get-tuple-element.21) | copy-start | bytes 4718596
  99.7 196.8 %all-gather.5.cloned.1.call-start = ((), (), s32[]{:S(2)}) async-start(), calls=%async_computation.1 | async-start | bytes 7077888 | tf_op jit(solution)/shard_map/all_gather | solution.py:127
  206.6 99.6 %copy-start.5 = (f32[32,768]{1,0:T(8,128)S(1)}, f32[32,768]{1,0:T(8,128)}, u32[]{:S(2)}) copy-start(f32[32,768]{1,0:T(8,128)} %param.7) | copy-start | bytes 294916
Sparse Core Ops, SparseCore 0:
  99.8 97.2 all-gather.6
  199.3 97.1 all-gather.4
